TPU v7x, 32 devices: a whole 2x2x4 slice. The times are simulated.
32 devices in a mesh: parts: 2 (over x), blk: 16 (over z, y, core).
Axes of the slice: x: 2, y: 2, z: 4, core: 2. Of those that a mesh axis runs over, the one named last changes fastest.
Arguments:
- observed: bfloat16 [24576, 1024], P(('parts', 'blk')), parts along dimension 0, may hold values from -6 to 6
- sharpness: float32 [24576], P(('parts', 'blk')), parts along dimension 0, may hold values from 0.03 to 0.15
- obs_class: int32 [24576], P(('parts', 'blk')), parts along dimension 0, may hold values from 0 to 7
- pattern: int32 [192, 16], P(('parts', 'blk')), parts along dimension 0, may hold values from 0 to 1, as said below
- evolved: bfloat16 [4096, 1024], P(('parts', 'blk')), parts along dimension 0, may hold values from -6 to 6
- sim_params: bfloat16 [4, 4096], P(None, ('parts', 'blk')), parts along dimension 1, may hold values from -6 to 6
- sim_class: int32 [4096], P(('parts', 'blk')), parts along dimension 0, may hold values from 0 to 7, as said below
Outputs:
- posterior_mean: float32 [4, 24576], P(None, ('parts', 'blk')), parts along dimension 1
- log_evidence: float32 [24576], P(('parts', 'blk')), parts along dimension 0
There are 2 independent parts, one for each index of `parts`. A program takes and returns all parts, laid end to end along the dimension named above; each array names one. Nothing has to cross between parts.
Inputs may be any that keep to these rules, and one draw needn't show every extreme that they name: `sim_class`: every block of 128 evolved profiles holds every class, at its first 8 positions. `pattern`: every block of observed profiles is compared with at least one block of evolved profiles; the share of compared blocks differs from one observed block to another.
All inputs are finite; a program needn't handle non-finite values.
Results may differ from a plain program's by a relative error of at most 0.0045.
Values may be sent and summed in bfloat16 or wider, within the bound.
A program may use at most 64 MiB of HBM per device.

v0:
```python
import jax
import jax.numpy as jnp
from jax import lax
from jax.sharding import PartitionSpec as P

NEG_START = -1e30


def from_behind(array, axis, by):
    count = lax.axis_size(axis)
    return lax.ppermute(array, axis, [(i, (i + by) % count) for i in range(count)])


def visit_block(
    observed,
    obs_sq,
    sharpness,
    obs_class,
    rows_open,
    sims,
    sims_sq,
    params,
    sims_class,
    running_max,
    weight_total,
    param_sums,
):
    inner = lax.dot_general(
        observed, sims, (((1,), (1,)), ((), ())), preferred_element_type=jnp.float32
    )
    distance = obs_sq[:, None] + sims_sq[None, :] - 2.0 * inner
    score = sharpness[:, None] * (2.0 * observed.shape[1] - distance)
    active = rows_open[:, None] & (obs_class[:, None] == sims_class[None, :])
    new_max = jnp.maximum(running_max, jnp.max(jnp.where(active, score, NEG_START), axis=1))
    factor = jnp.exp(running_max - new_max)
    weights = jnp.where(active, jnp.exp(score - new_max[:, None]), 0.0)
    weight_total = weight_total * factor + jnp.sum(weights, axis=1)
    weight_low = weights.astype(jnp.bfloat16)
    added = lax.dot_general(
        params, weight_low, (((1,), (1,)), ((), ())), preferred_element_type=jnp.float32
    )
    param_sums = param_sums * factor[None, :] + added
    return (new_max, weight_total, param_sums)


def on_device(observed, sharpness, obs_class, pattern, evolved, sim_params, sim_class):
    cycle_size = lax.axis_size("blk")
    position = lax.axis_index("blk")
    row_count = observed.shape[0]
    tile_count = pattern.shape[0]
    tile_rows = row_count // tile_count
    obs_sq = jnp.sum(jnp.square(observed.astype(jnp.float32)), axis=1)

    def absorb(state, packet, block_id):
        sims, params, class_low = packet
        sims_class = class_low.astype(jnp.int32)
        sims_sq = jnp.sum(jnp.square(sims.astype(jnp.float32)), axis=1)
        column = lax.dynamic_slice_in_dim(pattern, block_id, 1, 1)[:, 0] == 1
        rows_open = jnp.repeat(column, tile_rows)
        return visit_block(
            observed,
            obs_sq,
            sharpness,
            obs_class,
            rows_open,
            sims,
            sims_sq,
            params,
            sims_class,
            state[0],
            state[1],
            state[2],
        )

    packet = (evolved, sim_params, sim_class.astype(jnp.bfloat16))
    state = (
        jnp.full((row_count,), NEG_START, jnp.float32),
        jnp.zeros((row_count,), jnp.float32),
        jnp.zeros((sim_params.shape[0], row_count), jnp.float32),
    )
    state = absorb(state, packet, position)

    def turn(turn_index, carry):
        state_now, moving = carry
        moving = from_behind((moving[0], moving[1], moving[2]), "blk", 1)
        state_now = absorb(state_now, moving, (position - turn_index) % cycle_size)
        return (state_now, moving)

    state, packet_end = lax.fori_loop(1, cycle_size, turn, (state, packet))
    running_max, weight_total, param_sums = state
    return (param_sums / weight_total[None, :], running_max + jnp.log(weight_total))


def solution(mesh):
    placed = (
        P(("parts", "blk"), None),
        P(("parts", "blk")),
        P(("parts", "blk")),
        P(("parts", "blk"), None),
        P(("parts", "blk"), None),
        P(None, ("parts", "blk")),
        P(("parts", "blk")),
    )
    return jax.shard_map(
        on_device,
        mesh=mesh,
        in_specs=placed,
        out_specs=(P(None, ("parts", "blk")), P(("parts", "blk"))),
        check_vma=False,
    )
```

profile of v0, /device:TPU:0, one launch (start us, length us, event | category | flops | bytes accessed | tf_op | source)
XLA Modules:
  0.0 161.7 jit_solution(7447141425702174597)
XLA Ops:
  0.7 1.1 copy.33
  2.4 0.9 fusion.12
  4.2 1.8 %multiply_reduce_fusion.1 = f32[768]{0:T(1024)S(1)} fusion(bf16[768,1024]{1,0:T(8,128)(2,1)} %param.9), kind=kLoop, calls=%fused_computation.14 | loop fusion | flops 2358528 | bytes 1575936 | tf_op jit(solution)/shard_map/reduce_sum | solution.py:52
  7.2 153.3 %while.25 = (s32[]{:T(128)}, f32[768]{0:T(1024)S(1)}, f32[768]{0:T(1024)S(1)}, f32[4,768]{1,0:T(4,128)S(1)}, bf16[128,1024]{1,0:T(8,128)(2,1)S(1)}, /*index=5*/b...) while((s32[]{:T(128)}, f32[768]{0:T(1024)S(1)}, ...), condition=%wide.region_8.9_spmd, body=%wide.region_4.8_spmd.sunk | while | flops 205168144 | bytes 4967640 | solution.py:89
  7.7 2.6 %collective-permute-start.1 = (bf16[128]{0:T(256)(128)(2,1)S(1)}, bf16[128]{0:T(256)(128)(2,1)S(1)}, u32[]{:S(2)}, u32[]{:S(2)}) collective-permute-start(bf16[128]{0:T(256)(128)(2,1)S(1)} %get-tuple-element.475), channel_id=1, source_target_pairs={{0,1},{1,2},{2,3},{3,4},{4,5},{5,6},{6,7},{7,8},{8,9},{9,10},{10,1... | collective-permute-start | bytes 776 | tf_op jit(solution)/shard_map/while/body/eval_jaxpr/ppermute | solution.py:11
  10.4 6.3 %collective-permute-done.1 = bf16[128]{0:T(256)(128)(2,1)S(1)} collective-permute-done((bf16[128]{0:T(256)(128)(2,1)S(1)}, bf16[128]{0:T(256)(128)(2,1)S(1)}, u32[]{:S(2)}, u32[]{:S(2)}) %collective-permute-start.1) | collective-permute-done | bytes 288 | tf_op jit(solution)/shard_map/while/body/eval_jaxpr/ppermute | solution.py:11
  17.0 0.7 select_reduce_fusion.3
  18.6 8.3 %collective-permute-done.1 = bf16[128]{0:T(256)(128)(2,1)S(1)} collective-permute-done((bf16[128]{0:T(256)(128)(2,1)S(1)}, bf16[128]{0:T(256)(128)(2,1)S(1)}, u32[]{:S(2)}, u32[]{:S(2)}) %collective-permute-start.1) | collective-permute-done | bytes 288 | tf_op jit(solution)/shard_map/while/body/eval_jaxpr/ppermute | solution.py:11
  27.1 0.7 select_reduce_fusion.3
  28.8 8.3 %collective-permute-done.1 = bf16[128]{0:T(256)(128)(2,1)S(1)} collective-permute-done((bf16[128]{0:T(256)(128)(2,1)S(1)}, bf16[128]{0:T(256)(128)(2,1)S(1)}, u32[]{:S(2)}, u32[]{:S(2)}) %collective-permute-start.1) | collective-permute-done | bytes 288 | tf_op jit(solution)/shard_map/while/body/eval_jaxpr/ppermute | solution.py:11
  37.3 0.7 select_reduce_fusion.3
  39.0 8.3 %collective-permute-done.1 = bf16[128]{0:T(256)(128)(2,1)S(1)} collective-permute-done((bf16[128]{0:T(256)(128)(2,1)S(1)}, bf16[128]{0:T(256)(128)(2,1)S(1)}, u32[]{:S(2)}, u32[]{:S(2)}) %collective-permute-start.1) | collective-permute-done | bytes 288 | tf_op jit(solution)/shard_map/while/body/eval_jaxpr/ppermute | solution.py:11
  47.4 0.7 select_reduce_fusion.3
  49.1 8.3 %collective-permute-done.1 = bf16[128]{0:T(256)(128)(2,1)S(1)} collective-permute-done((bf16[128]{0:T(256)(128)(2,1)S(1)}, bf16[128]{0:T(256)(128)(2,1)S(1)}, u32[]{:S(2)}, u32[]{:S(2)}) %collective-permute-start.1) | collective-permute-done | bytes 288 | tf_op jit(solution)/shard_map/while/body/eval_jaxpr/ppermute | solution.py:11
  57.6 0.7 select_reduce_fusion.3
  59.3 8.3 %collective-permute-done.1 = bf16[128]{0:T(256)(128)(2,1)S(1)} collective-permute-done((bf16[128]{0:T(256)(128)(2,1)S(1)}, bf16[128]{0:T(256)(128)(2,1)S(1)}, u32[]{:S(2)}, u32[]{:S(2)}) %collective-permute-start.1) | collective-permute-done | bytes 288 | tf_op jit(solution)/shard_map/while/body/eval_jaxpr/ppermute | solution.py:11
  67.7 0.7 select_reduce_fusion.3
  69.4 8.3 %collective-permute-done.1 = bf16[128]{0:T(256)(128)(2,1)S(1)} collective-permute-done((bf16[128]{0:T(256)(128)(2,1)S(1)}, bf16[128]{0:T(256)(128)(2,1)S(1)}, u32[]{:S(2)}, u32[]{:S(2)}) %collective-permute-start.1) | collective-permute-done | bytes 288 | tf_op jit(solution)/shard_map/while/body/eval_jaxpr/ppermute | solution.py:11
  77.9 0.7 select_reduce_fusion.3
  79.6 8.3 %collective-permute-done.1 = bf16[128]{0:T(256)(128)(2,1)S(1)} collective-permute-done((bf16[128]{0:T(256)(128)(2,1)S(1)}, bf16[128]{0:T(256)(128)(2,1)S(1)}, u32[]{:S(2)}, u32[]{:S(2)}) %collective-permute-start.1) | collective-permute-done | bytes 288 | tf_op jit(solution)/shard_map/while/body/eval_jaxpr/ppermute | solution.py:11
  88.0 0.7 select_reduce_fusion.3
  89.7 8.3 %collective-permute-done.1 = bf16[128]{0:T(256)(128)(2,1)S(1)} collective-permute-done((bf16[128]{0:T(256)(128)(2,1)S(1)}, bf16[128]{0:T(256)(128)(2,1)S(1)}, u32[]{:S(2)}, u32[]{:S(2)}) %collective-permute-start.1) | collective-permute-done | bytes 288 | tf_op jit(solution)/shard_map/while/body/eval_jaxpr/ppermute | solution.py:11
  98.2 0.7 select_reduce_fusion.3
  99.9 8.3 %collective-permute-done.1 = bf16[128]{0:T(256)(128)(2,1)S(1)} collective-permute-done((bf16[128]{0:T(256)(128)(2,1)S(1)}, bf16[128]{0:T(256)(128)(2,1)S(1)}, u32[]{:S(2)}, u32[]{:S(2)}) %collective-permute-start.1) | collective-permute-done | bytes 288 | tf_op jit(solution)/shard_map/while/body/eval_jaxpr/ppermute | solution.py:11
  108.4 0.7 select_reduce_fusion.3
  110.0 8.3 %collective-permute-done.1 = bf16[128]{0:T(256)(128)(2,1)S(1)} collective-permute-done((bf16[128]{0:T(256)(128)(2,1)S(1)}, bf16[128]{0:T(256)(128)(2,1)S(1)}, u32[]{:S(2)}, u32[]{:S(2)}) %collective-permute-start.1) | collective-permute-done | bytes 288 | tf_op jit(solution)/shard_map/while/body/eval_jaxpr/ppermute | solution.py:11
  118.5 0.7 select_reduce_fusion.3
  120.2 8.3 %collective-permute-done.1 = bf16[128]{0:T(256)(128)(2,1)S(1)} collective-permute-done((bf16[128]{0:T(256)(128)(2,1)S(1)}, bf16[128]{0:T(256)(128)(2,1)S(1)}, u32[]{:S(2)}, u32[]{:S(2)}) %collective-permute-start.1) | collective-permute-done | bytes 288 | tf_op jit(solution)/shard_map/while/body/eval_jaxpr/ppermute | solution.py:11
  128.7 0.7 select_reduce_fusion.3
  130.4 8.3 %collective-permute-done.1 = bf16[128]{0:T(256)(128)(2,1)S(1)} collective-permute-done((bf16[128]{0:T(256)(128)(2,1)S(1)}, bf16[128]{0:T(256)(128)(2,1)S(1)}, u32[]{:S(2)}, u32[]{:S(2)}) %collective-permute-start.1) | collective-permute-done | bytes 288 | tf_op jit(solution)/shard_map/while/body/eval_jaxpr/ppermute | solution.py:11
  140.5 8.3 %collective-permute-done.1 = bf16[128]{0:T(256)(128)(2,1)S(1)} collective-permute-done((bf16[128]{0:T(256)(128)(2,1)S(1)}, bf16[128]{0:T(256)(128)(2,1)S(1)}, u32[]{:S(2)}, u32[]{:S(2)}) %collective-permute-start.1) | collective-permute-done | bytes 288 | tf_op jit(solution)/shard_map/while/body/eval_jaxpr/ppermute | solution.py:11
  150.7 8.3 %collective-permute-done.1 = bf16[128]{0:T(256)(128)(2,1)S(1)} collective-permute-done((bf16[128]{0:T(256)(128)(2,1)S(1)}, bf16[128]{0:T(256)(128)(2,1)S(1)}, u32[]{:S(2)}, u32[]{:S(2)}) %collective-permute-start.1) | collective-permute-done | bytes 288 | tf_op jit(solution)/shard_map/while/body/eval_jaxpr/ppermute | solution.py:11
  (277 shorter events, 22.0 us)
Async XLA Ops:
  7.2 9.6 %collective-permute-start = (bf16[128,1024]{1,0:T(8,128)(2,1)S(1)}, bf16[128,1024]{1,0:T(8,128)(2,1)S(1)}, u32[]{:S(2)}, u32[]{:S(2)}) collective-permute-start(bf16[128,1024]{1,0:T(8,128)(2,1)S(1)} %get-tuple-element.473), channel_id=1, source_target_pairs={{0,1},{1,2},{2,3},{3,4},{4,5},{5,6},{6,7},{7,8},{8,9},{9,10},{10,1... | collective-permute-start | bytes 786440 | tf_op jit(solution)/shard_map/while/body/eval_jaxpr/ppermute | solution.py:11
  7.7 9.1 %collective-permute-start.1 = (bf16[128]{0:T(256)(128)(2,1)S(1)}, bf16[128]{0:T(256)(128)(2,1)S(1)}, u32[]{:S(2)}, u32[]{:S(2)}) collective-permute-start(bf16[128]{0:T(256)(128)(2,1)S(1)} %get-tuple-element.475), channel_id=1, source_target_pairs={{0,1},{1,2},{2,3},{3,4},{4,5},{5,6},{6,7},{7,8},{8,9},{9,10},{10,1... | collective-permute-start | bytes 776 | tf_op jit(solution)/shard_map/while/body/eval_jaxpr/ppermute | solution.py:11
  18.3 8.6 %collective-permute-start = (bf16[128,1024]{1,0:T(8,128)(2,1)S(1)}, bf16[128,1024]{1,0:T(8,128)(2,1)S(1)}, u32[]{:S(2)}, u32[]{:S(2)}) collective-permute-start(bf16[128,1024]{1,0:T(8,128)(2,1)S(1)} %get-tuple-element.473), channel_id=1, source_target_pairs={{0,1},{1,2},{2,3},{3,4},{4,5},{5,6},{6,7},{7,8},{8,9},{9,10},{10,1... | collective-permute-start | bytes 786440 | tf_op jit(solution)/shard_map/while/body/eval_jaxpr/ppermute | solution.py:11
  18.4 8.5 %collective-permute-start.1 = (bf16[128]{0:T(256)(128)(2,1)S(1)}, bf16[128]{0:T(256)(128)(2,1)S(1)}, u32[]{:S(2)}, u32[]{:S(2)}) collective-permute-start(bf16[128]{0:T(256)(128)(2,1)S(1)} %get-tuple-element.475), channel_id=1, source_target_pairs={{0,1},{1,2},{2,3},{3,4},{4,5},{5,6},{6,7},{7,8},{8,9},{9,10},{10,1... | collective-permute-start | bytes 776 | tf_op jit(solution)/shard_map/while/body/eval_jaxpr/ppermute | solution.py:11
  18.5 8.5 %collective-permute-start.2 = (bf16[4,128]{1,0:T(4,128)(2,1)S(1)}, bf16[4,128]{1,0:T(4,128)(2,1)S(1)}, u32[]{:S(2)}, u32[]{:S(2)}) collective-permute-start(bf16[4,128]{1,0:T(4,128)(2,1)S(1)} %get-tuple-element.474), channel_id=1, source_target_pairs={{0,1},{1,2},{2,3},{3,4},{4,5},{5,6},{6,7},{7,8},{8,9},{9,10},{10,1... | collective-permute-start | bytes 3080 | tf_op jit(solution)/shard_map/while/body/eval_jaxpr/ppermute | solution.py:11
  28.5 8.6 %collective-permute-start = (bf16[128,1024]{1,0:T(8,128)(2,1)S(1)}, bf16[128,1024]{1,0:T(8,128)(2,1)S(1)}, u32[]{:S(2)}, u32[]{:S(2)}) collective-permute-start(bf16[128,1024]{1,0:T(8,128)(2,1)S(1)} %get-tuple-element.473), channel_id=1, source_target_pairs={{0,1},{1,2},{2,3},{3,4},{4,5},{5,6},{6,7},{7,8},{8,9},{9,10},{10,1... | collective-permute-start | bytes 786440 | tf_op jit(solution)/shard_map/while/body/eval_jaxpr/ppermute | solution.py:11
  28.6 8.5 %collective-permute-start.1 = (bf16[128]{0:T(256)(128)(2,1)S(1)}, bf16[128]{0:T(256)(128)(2,1)S(1)}, u32[]{:S(2)}, u32[]{:S(2)}) collective-permute-start(bf16[128]{0:T(256)(128)(2,1)S(1)} %get-tuple-element.475), channel_id=1, source_target_pairs={{0,1},{1,2},{2,3},{3,4},{4,5},{5,6},{6,7},{7,8},{8,9},{9,10},{10,1... | collective-permute-start | bytes 776 | tf_op jit(solution)/shard_map/while/body/eval_jaxpr/ppermute | solution.py:11
  38.6 8.6 %collective-permute-start = (bf16[128,1024]{1,0:T(8,128)(2,1)S(1)}, bf16[128,1024]{1,0:T(8,128)(2,1)S(1)}, u32[]{:S(2)}, u32[]{:S(2)}) collective-permute-start(bf16[128,1024]{1,0:T(8,128)(2,1)S(1)} %get-tuple-element.473), channel_id=1, source_target_pairs={{0,1},{1,2},{2,3},{3,4},{4,5},{5,6},{6,7},{7,8},{8,9},{9,10},{10,1... | collective-permute-start | bytes 786440 | tf_op jit(solution)/shard_map/while/body/eval_jaxpr/ppermute | solution.py:11
  38.7 8.5 %collective-permute-start.1 = (bf16[128]{0:T(256)(128)(2,1)S(1)}, bf16[128]{0:T(256)(128)(2,1)S(1)}, u32[]{:S(2)}, u32[]{:S(2)}) collective-permute-start(bf16[128]{0:T(256)(128)(2,1)S(1)} %get-tuple-element.475), channel_id=1, source_target_pairs={{0,1},{1,2},{2,3},{3,4},{4,5},{5,6},{6,7},{7,8},{8,9},{9,10},{10,1... | collective-permute-start | bytes 776 | tf_op jit(solution)/shard_map/while/body/eval_jaxpr/ppermute | solution.py:11
  48.8 8.6 %collective-permute-start = (bf16[128,1024]{1,0:T(8,128)(2,1)S(1)}, bf16[128,1024]{1,0:T(8,128)(2,1)S(1)}, u32[]{:S(2)}, u32[]{:S(2)}) collective-permute-start(bf16[128,1024]{1,0:T(8,128)(2,1)S(1)} %get-tuple-element.473), channel_id=1, source_target_pairs={{0,1},{1,2},{2,3},{3,4},{4,5},{5,6},{6,7},{7,8},{8,9},{9,10},{10,1... | collective-permute-start | bytes 786440 | tf_op jit(solution)/shard_map/while/body/eval_jaxpr/ppermute | solution.py:11
  48.9 8.5 %collective-permute-start.1 = (bf16[128]{0:T(256)(128)(2,1)S(1)}, bf16[128]{0:T(256)(128)(2,1)S(1)}, u32[]{:S(2)}, u32[]{:S(2)}) collective-permute-start(bf16[128]{0:T(256)(128)(2,1)S(1)} %get-tuple-element.475), channel_id=1, source_target_pairs={{0,1},{1,2},{2,3},{3,4},{4,5},{5,6},{6,7},{7,8},{8,9},{9,10},{10,1... | collective-permute-start | bytes 776 | tf_op jit(solution)/shard_map/while/body/eval_jaxpr/ppermute | solution.py:11
  59.0 8.6 %collective-permute-start = (bf16[128,1024]{1,0:T(8,128)(2,1)S(1)}, bf16[128,1024]{1,0:T(8,128)(2,1)S(1)}, u32[]{:S(2)}, u32[]{:S(2)}) collective-permute-start(bf16[128,1024]{1,0:T(8,128)(2,1)S(1)} %get-tuple-element.473), channel_id=1, source_target_pairs={{0,1},{1,2},{2,3},{3,4},{4,5},{5,6},{6,7},{7,8},{8,9},{9,10},{10,1... | collective-permute-start | bytes 786440 | tf_op jit(solution)/shard_map/while/body/eval_jaxpr/ppermute | solution.py:11
  59.0 8.5 %collective-permute-start.1 = (bf16[128]{0:T(256)(128)(2,1)S(1)}, bf16[128]{0:T(256)(128)(2,1)S(1)}, u32[]{:S(2)}, u32[]{:S(2)}) collective-permute-start(bf16[128]{0:T(256)(128)(2,1)S(1)} %get-tuple-element.475), channel_id=1, source_target_pairs={{0,1},{1,2},{2,3},{3,4},{4,5},{5,6},{6,7},{7,8},{8,9},{9,10},{10,1... | collective-permute-start | bytes 776 | tf_op jit(solution)/shard_map/while/body/eval_jaxpr/ppermute | solution.py:11
  69.1 8.6 %collective-permute-start = (bf16[128,1024]{1,0:T(8,128)(2,1)S(1)}, bf16[128,1024]{1,0:T(8,128)(2,1)S(1)}, u32[]{:S(2)}, u32[]{:S(2)}) collective-permute-start(bf16[128,1024]{1,0:T(8,128)(2,1)S(1)} %get-tuple-element.473), channel_id=1, source_target_pairs={{0,1},{1,2},{2,3},{3,4},{4,5},{5,6},{6,7},{7,8},{8,9},{9,10},{10,1... | collective-permute-start | bytes 786440 | tf_op jit(solution)/shard_map/while/body/eval_jaxpr/ppermute | solution.py:11
  69.2 8.5 %collective-permute-start.1 = (bf16[128]{0:T(256)(128)(2,1)S(1)}, bf16[128]{0:T(256)(128)(2,1)S(1)}, u32[]{:S(2)}, u32[]{:S(2)}) collective-permute-start(bf16[128]{0:T(256)(128)(2,1)S(1)} %get-tuple-element.475), channel_id=1, source_target_pairs={{0,1},{1,2},{2,3},{3,4},{4,5},{5,6},{6,7},{7,8},{8,9},{9,10},{10,1... | collective-permute-start | bytes 776 | tf_op jit(solution)/shard_map/while/body/eval_jaxpr/ppermute | solution.py:11
  79.3 8.6 %collective-permute-start = (bf16[128,1024]{1,0:T(8,128)(2,1)S(1)}, bf16[128,1024]{1,0:T(8,128)(2,1)S(1)}, u32[]{:S(2)}, u32[]{:S(2)}) collective-permute-start(bf16[128,1024]{1,0:T(8,128)(2,1)S(1)} %get-tuple-element.473), channel_id=1, source_target_pairs={{0,1},{1,2},{2,3},{3,4},{4,5},{5,6},{6,7},{7,8},{8,9},{9,10},{10,1... | collective-permute-start | bytes 786440 | tf_op jit(solution)/shard_map/while/body/eval_jaxpr/ppermute | solution.py:11
  79.3 8.5 %collective-permute-start.1 = (bf16[128]{0:T(256)(128)(2,1)S(1)}, bf16[128]{0:T(256)(128)(2,1)S(1)}, u32[]{:S(2)}, u32[]{:S(2)}) collective-permute-start(bf16[128]{0:T(256)(128)(2,1)S(1)} %get-tuple-element.475), channel_id=1, source_target_pairs={{0,1},{1,2},{2,3},{3,4},{4,5},{5,6},{6,7},{7,8},{8,9},{9,10},{10,1... | collective-permute-start | bytes 776 | tf_op jit(solution)/shard_map/while/body/eval_jaxpr/ppermute | solution.py:11
  89.4 8.6 %collective-permute-start = (bf16[128,1024]{1,0:T(8,128)(2,1)S(1)}, bf16[128,1024]{1,0:T(8,128)(2,1)S(1)}, u32[]{:S(2)}, u32[]{:S(2)}) collective-permute-start(bf16[128,1024]{1,0:T(8,128)(2,1)S(1)} %get-tuple-element.473), channel_id=1, source_target_pairs={{0,1},{1,2},{2,3},{3,4},{4,5},{5,6},{6,7},{7,8},{8,9},{9,10},{10,1... | collective-permute-start | bytes 786440 | tf_op jit(solution)/shard_map/while/body/eval_jaxpr/ppermute | solution.py:11
  89.5 8.5 %collective-permute-start.1 = (bf16[128]{0:T(256)(128)(2,1)S(1)}, bf16[128]{0:T(256)(128)(2,1)S(1)}, u32[]{:S(2)}, u32[]{:S(2)}) collective-permute-start(bf16[128]{0:T(256)(128)(2,1)S(1)} %get-tuple-element.475), channel_id=1, source_target_pairs={{0,1},{1,2},{2,3},{3,4},{4,5},{5,6},{6,7},{7,8},{8,9},{9,10},{10,1... | collective-permute-start | bytes 776 | tf_op jit(solution)/shard_map/while/body/eval_jaxpr/ppermute | solution.py:11
  99.6 8.6 %collective-permute-start = (bf16[128,1024]{1,0:T(8,128)(2,1)S(1)}, bf16[128,1024]{1,0:T(8,128)(2,1)S(1)}, u32[]{:S(2)}, u32[]{:S(2)}) collective-permute-start(bf16[128,1024]{1,0:T(8,128)(2,1)S(1)} %get-tuple-element.473), channel_id=1, source_target_pairs={{0,1},{1,2},{2,3},{3,4},{4,5},{5,6},{6,7},{7,8},{8,9},{9,10},{10,1... | collective-permute-start | bytes 786440 | tf_op jit(solution)/shard_map/while/body/eval_jaxpr/ppermute | solution.py:11
  99.6 8.5 %collective-permute-start.1 = (bf16[128]{0:T(256)(128)(2,1)S(1)}, bf16[128]{0:T(256)(128)(2,1)S(1)}, u32[]{:S(2)}, u32[]{:S(2)}) collective-permute-start(bf16[128]{0:T(256)(128)(2,1)S(1)} %get-tuple-element.475), channel_id=1, source_target_pairs={{0,1},{1,2},{2,3},{3,4},{4,5},{5,6},{6,7},{7,8},{8,9},{9,10},{10,1... | collective-permute-start | bytes 776 | tf_op jit(solution)/shard_map/while/body/eval_jaxpr/ppermute | solution.py:11
  109.7 8.6 %collective-permute-start = (bf16[128,1024]{1,0:T(8,128)(2,1)S(1)}, bf16[128,1024]{1,0:T(8,128)(2,1)S(1)}, u32[]{:S(2)}, u32[]{:S(2)}) collective-permute-start(bf16[128,1024]{1,0:T(8,128)(2,1)S(1)} %get-tuple-element.473), channel_id=1, source_target_pairs={{0,1},{1,2},{2,3},{3,4},{4,5},{5,6},{6,7},{7,8},{8,9},{9,10},{10,1... | collective-permute-start | bytes 786440 | tf_op jit(solution)/shard_map/while/body/eval_jaxpr/ppermute | solution.py:11
  109.8 8.5 %collective-permute-start.1 = (bf16[128]{0:T(256)(128)(2,1)S(1)}, bf16[128]{0:T(256)(128)(2,1)S(1)}, u32[]{:S(2)}, u32[]{:S(2)}) collective-permute-start(bf16[128]{0:T(256)(128)(2,1)S(1)} %get-tuple-element.475), channel_id=1, source_target_pairs={{0,1},{1,2},{2,3},{3,4},{4,5},{5,6},{6,7},{7,8},{8,9},{9,10},{10,1... | collective-permute-start | bytes 776 | tf_op jit(solution)/shard_map/while/body/eval_jaxpr/ppermute | solution.py:11
  119.9 8.6 %collective-permute-start = (bf16[128,1024]{1,0:T(8,128)(2,1)S(1)}, bf16[128,1024]{1,0:T(8,128)(2,1)S(1)}, u32[]{:S(2)}, u32[]{:S(2)}) collective-permute-start(bf16[128,1024]{1,0:T(8,128)(2,1)S(1)} %get-tuple-element.473), channel_id=1, source_target_pairs={{0,1},{1,2},{2,3},{3,4},{4,5},{5,6},{6,7},{7,8},{8,9},{9,10},{10,1... | collective-permute-start | bytes 786440 | tf_op jit(solution)/shard_map/while/body/eval_jaxpr/ppermute | solution.py:11
  120.0 8.5 %collective-permute-start.1 = (bf16[128]{0:T(256)(128)(2,1)S(1)}, bf16[128]{0:T(256)(128)(2,1)S(1)}, u32[]{:S(2)}, u32[]{:S(2)}) collective-permute-start(bf16[128]{0:T(256)(128)(2,1)S(1)} %get-tuple-element.475), channel_id=1, source_target_pairs={{0,1},{1,2},{2,3},{3,4},{4,5},{5,6},{6,7},{7,8},{8,9},{9,10},{10,1... | collective-permute-start | bytes 776 | tf_op jit(solution)/shard_map/while/body/eval_jaxpr/ppermute | solution.py:11
  130.0 8.6 %collective-permute-start = (bf16[128,1024]{1,0:T(8,128)(2,1)S(1)}, bf16[128,1024]{1,0:T(8,128)(2,1)S(1)}, u32[]{:S(2)}, u32[]{:S(2)}) collective-permute-start(bf16[128,1024]{1,0:T(8,128)(2,1)S(1)} %get-tuple-element.473), channel_id=1, source_target_pairs={{0,1},{1,2},{2,3},{3,4},{4,5},{5,6},{6,7},{7,8},{8,9},{9,10},{10,1... | collective-permute-start | bytes 786440 | tf_op jit(solution)/shard_map/while/body/eval_jaxpr/ppermute | solution.py:11
  130.1 8.5 %collective-permute-start.1 = (bf16[128]{0:T(256)(128)(2,1)S(1)}, bf16[128]{0:T(256)(128)(2,1)S(1)}, u32[]{:S(2)}, u32[]{:S(2)}) collective-permute-start(bf16[128]{0:T(256)(128)(2,1)S(1)} %get-tuple-element.475), channel_id=1, source_target_pairs={{0,1},{1,2},{2,3},{3,4},{4,5},{5,6},{6,7},{7,8},{8,9},{9,10},{10,1... | collective-permute-start | bytes 776 | tf_op jit(solution)/shard_map/while/body/eval_jaxpr/ppermute | solution.py:11
  140.2 8.6 %collective-permute-start = (bf16[128,1024]{1,0:T(8,128)(2,1)S(1)}, bf16[128,1024]{1,0:T(8,128)(2,1)S(1)}, u32[]{:S(2)}, u32[]{:S(2)}) collective-permute-start(bf16[128,1024]{1,0:T(8,128)(2,1)S(1)} %get-tuple-element.473), channel_id=1, source_target_pairs={{0,1},{1,2},{2,3},{3,4},{4,5},{5,6},{6,7},{7,8},{8,9},{9,10},{10,1... | collective-permute-start | bytes 786440 | tf_op jit(solution)/shard_map/while/body/eval_jaxpr/ppermute | solution.py:11
  140.3 8.5 %collective-permute-start.1 = (bf16[128]{0:T(256)(128)(2,1)S(1)}, bf16[128]{0:T(256)(128)(2,1)S(1)}, u32[]{:S(2)}, u32[]{:S(2)}) collective-permute-start(bf16[128]{0:T(256)(128)(2,1)S(1)} %get-tuple-element.475), channel_id=1, source_target_pairs={{0,1},{1,2},{2,3},{3,4},{4,5},{5,6},{6,7},{7,8},{8,9},{9,10},{10,1... | collective-permute-start | bytes 776 | tf_op jit(solution)/shard_map/while/body/eval_jaxpr/ppermute | solution.py:11
  140.3 8.5 %collective-permute-start.2 = (bf16[4,128]{1,0:T(4,128)(2,1)S(1)}, bf16[4,128]{1,0:T(4,128)(2,1)S(1)}, u32[]{:S(2)}, u32[]{:S(2)}) collective-permute-start(bf16[4,128]{1,0:T(4,128)(2,1)S(1)} %get-tuple-element.474), channel_id=1, source_target_pairs={{0,1},{1,2},{2,3},{3,4},{4,5},{5,6},{6,7},{7,8},{8,9},{9,10},{10,1... | collective-permute-start | bytes 3080 | tf_op jit(solution)/shard_map/while/body/eval_jaxpr/ppermute | solution.py:11
  150.4 8.6 %collective-permute-start = (bf16[128,1024]{1,0:T(8,128)(2,1)S(1)}, bf16[128,1024]{1,0:T(8,128)(2,1)S(1)}, u32[]{:S(2)}, u32[]{:S(2)}) collective-permute-start(bf16[128,1024]{1,0:T(8,128)(2,1)S(1)} %get-tuple-element.473), channel_id=1, source_target_pairs={{0,1},{1,2},{2,3},{3,4},{4,5},{5,6},{6,7},{7,8},{8,9},{9,10},{10,1... | collective-permute-start | bytes 786440 | tf_op jit(solution)/shard_map/while/body/eval_jaxpr/ppermute | solution.py:11
  150.4 8.5 %collective-permute-start.1 = (bf16[128]{0:T(256)(128)(2,1)S(1)}, bf16[128]{0:T(256)(128)(2,1)S(1)}, u32[]{:S(2)}, u32[]{:S(2)}) collective-permute-start(bf16[128]{0:T(256)(128)(2,1)S(1)} %get-tuple-element.475), channel_id=1, source_target_pairs={{0,1},{1,2},{2,3},{3,4},{4,5},{5,6},{6,7},{7,8},{8,9},{9,10},{10,1... | collective-permute-start | bytes 776 | tf_op jit(solution)/shard_map/while/body/eval_jaxpr/ppermute | solution.py:11
  (17 other events, 125.4 us)
where the time goes:
time: 162 us
  waiting for transfers between devices  123 us (76%)
  matrix products  16.7 us (10%)
  other arithmetic  11.1 us (7%)
  starting transfers between devices  5.54 us (3%)
  local copies, waits for them, and re-layouts  3.43 us (2%)
  loops' own time  1.73 us (1%)
    ppermute x45, waiting for transfers between devices, from_behind(): lax.ppermute(array, axis, [(i, (i + by) % count) for i in range(count)])  123 us
    dot_general x16, matrix products, visit_block(): lax.dot_general(observed, sims, (((1,), (1,)), ((), ())), preferred_eleme...  11.4 us
    ppermute x45, starting transfers between devices, from_behind(): lax.ppermute(array, axis, [(i, (i + by) % count) for i in range(count)])  5.54 us
    dot_general x16, matrix products, visit_block(): lax.dot_general(params, weight_low, (((1,), (1,)), ((), ())), preferred_e...  5.37 us
    reduce_sum x16, other arithmetic, visit_block(): weight_total = weight_total * factor + jnp.sum(weights, axis=1)  3.88 us
  transfers between devices with their start and end apart: 45, of which 15 were waited for; matrix products, arithmetic and copies ran while one was open for 1% of the time, Pallas kernels for 0%

commit v1 on v0

v1 whole, which is shorter than its diff:
```python
import functools

import jax
import jax.numpy as jnp
from jax import lax
from jax.experimental import pallas as pl
from jax.experimental.pallas import tpu as pltpu
from jax.sharding import PartitionSpec as P

NEG_START = -1e30
NEG_MASK = -3e38
LANES = 128
AUX_ROWS = 16
MESH = pl.DeviceIdType.MESH


def kernel(
    depth,
    obs_hbm,
    sharp_ref,
    ocls_ref,
    pat_ref,
    evo_hbm,
    prm_ref,
    scls_ref,
    mean_ref,
    lev_ref,
    gat,
    obs,
    evo,
    stage,
    base_sc,
    max_sc,
    tot_sc,
    sum_sc,
    local_sem,
    up_send,
    dn_send,
    y_send,
    s_send,
    z_recv,
    y_recv,
    s_recv,
):
    me = lax.axis_index("blk")
    z, y, c = me // 4, (me // 2) % 2, me % 2
    rows, feat = obs.shape
    sims = evo.shape[0]
    tiles = feat // LANES
    tile_count = pat_ref.shape[0]
    tile_rows = rows // tile_count
    nparam = prm_ref.shape[0]

    def blk_of(zz, yy, cc):
        return zz * 4 + yy * 2 + cc

    evo_copy = pltpu.make_async_copy(evo_hbm, evo, local_sem.at[0])
    obs_copy = pltpu.make_async_copy(obs_hbm, obs, local_sem.at[1])
    evo_copy.start()
    obs_copy.start()

    has_up = z < depth - 1
    has_dn = z > 0

    barrier = pltpu.get_barrier_semaphore()

    def greet(dev):
        pl.semaphore_signal(barrier, inc=1, device_id={"blk": dev}, device_id_type=MESH)

    greet(blk_of(z, y, 1 - c))
    greet(blk_of(z, 1 - y, c))

    @pl.when(has_up)
    def _():
        greet(blk_of(z + 1, y, c))

    @pl.when(has_dn)
    def _():
        greet(blk_of(z - 1, y, c))

    stage[...] = jnp.zeros_like(stage)
    stage[0:nparam, :] = prm_ref[...].astype(jnp.float32)
    stage[nparam : nparam + 1, :] = scls_ref[...].astype(jnp.float32)
    evo_copy.wait()
    for t in range(tiles):
        gat[z, y, c, t * sims : (t + 1) * sims, :] = evo[:, t * LANES : (t + 1) * LANES]
    gat[z, y, c, tiles * sims : tiles * sims + AUX_ROWS, :] = stage[...].astype(jnp.bfloat16)

    peers = 2 + (z + depth - 1) // depth + (2 * depth - 2 - z) // depth
    pl.semaphore_wait(barrier, peers)

    def packet(o, yy, cc, dev, send, recv):
        return pltpu.make_async_remote_copy(
            src_ref=gat.at[o, yy, cc],
            dst_ref=gat.at[o, yy, cc],
            send_sem=send,
            recv_sem=recv,
            device_id={"blk": dev},
            device_id_type=MESH,
        )

    def to_up(o):
        return packet(o, y, c, blk_of(z + 1, y, c), up_send.at[o], z_recv.at[o])

    def to_dn(o):
        return packet(o, y, c, blk_of(z - 1, y, c), dn_send.at[o], z_recv.at[o])

    def to_y(o):
        return packet(o, y, c, blk_of(z, 1 - y, c), y_send.at[o], y_recv.at[o])

    def from_y(o):
        return packet(o, 1 - y, c, blk_of(z, 1 - y, c), y_send.at[o], y_recv.at[o])

    def to_core(o, yy):
        return packet(
            o, yy, c, blk_of(z, y, 1 - c), s_send.at[o * 2 + yy], s_recv.at[o * 2 + yy]
        )

    def from_core(o, yy):
        return packet(
            o, yy, 1 - c, blk_of(z, y, 1 - c), s_send.at[o * 2 + yy], s_recv.at[o * 2 + yy]
        )

    @pl.when(has_up)
    def _():
        to_up(z).start()

    @pl.when(has_dn)
    def _():
        to_dn(z).start()

    to_y(z).start()
    to_core(z, y).start()

    obs_copy.wait()
    for i in range(rows // LANES):
        part = obs[i * LANES : (i + 1) * LANES, :].astype(jnp.float32)
        col = jnp.sum(part * part, axis=1, keepdims=True)
        wide = jnp.broadcast_to(col, (LANES, LANES)).T
        base_sc[0:1, i * LANES : (i + 1) * LANES] = 1.0 * feat - 0.5 * wide[0:1, :]

    max_sc[...] = jnp.full_like(max_sc, NEG_START)
    tot_sc[...] = jnp.zeros_like(tot_sc)
    sum_sc[...] = jnp.zeros_like(sum_sc)
    group = 2 if tile_count % 2 == 0 else 1
    width = group * tile_rows

    def absorb(o, yy):
        lhs, half_sq, classes, aux = [], [], [], []
        for cc in range(2):
            block = jnp.concatenate(
                [gat[o, yy, cc, t * sims : (t + 1) * sims, :] for t in range(tiles)], axis=1
            )
            wide = block.astype(jnp.float32)
            half_sq.append(0.5 * jnp.sum(wide * wide, axis=1, keepdims=True))
            extra = gat[o, yy, cc, tiles * sims : tiles * sims + AUX_ROWS, :]
            row = extra.astype(jnp.float32)[nparam : nparam + 1, :]
            turned = jnp.broadcast_to(row, (LANES, LANES)).T
            classes.append(turned[:, 0:1])
            aux.append(extra)
            lhs.append(block)
        lhs = jnp.concatenate(lhs, axis=0)
        for g in range(tile_count // group):
            span = slice(g * width, (g + 1) * width)
            inner = lax.dot_general(
                lhs, obs[span, :], (((1,), (1,)), ((), ())), preferred_element_type=jnp.float32
            )
            sharp2 = 2.0 * sharp_ref[0:1, span]
            base = base_sc[0:1, span]
            masked = []
            for cc in range(2):
                wanted = jnp.concatenate(
                    [
                        jnp.where(
                            pat_ref[i, blk_of(o, yy, cc)] == 1,
                            ocls_ref[0:1, i * tile_rows : (i + 1) * tile_rows],
                            -1,
                        )
                        for i in range(g * group, (g + 1) * group)
                    ],
                    axis=1,
                ).astype(jnp.float32)
                score = ((inner[cc * sims : (cc + 1) * sims] - half_sq[cc]) + base) * sharp2
                masked.append(jnp.where(classes[cc] == wanted, score, NEG_MASK))
            top = jnp.max(jnp.maximum(masked[0], masked[1]), axis=0, keepdims=True)
            old = max_sc[0:1, span]
            new = jnp.maximum(old, top)
            factor = jnp.exp(old - new)
            w0 = jnp.exp(masked[0] - new)
            w1 = jnp.exp(masked[1] - new)
            max_sc[0:1, span] = new
            tot_sc[0:1, span] = tot_sc[0:1, span] * factor + jnp.sum(
                w0 + w1, axis=0, keepdims=True
            )
            added = lax.dot_general(
                jnp.concatenate(aux, axis=1),
                jnp.concatenate([w0, w1], axis=0).astype(jnp.bfloat16),
                (((1,), (0,)), ((), ())),
                preferred_element_type=jnp.float32,
            )
            sum_sc[:, span] = sum_sc[:, span] * factor + added

    def step(s, carry):
        lo, hi = z - s, z + s
        has_lo, has_hi = lo >= 0, hi < depth
        lo_y, hi_y = z - s + 1, z + s - 1
        has_lo_y = lo_y >= 0
        has_hi_y = (hi_y < depth) & (s > 1)

        @pl.when(has_lo)
        def _():
            to_up(lo).wait_recv()

            @pl.when(has_up)
            def _():
                to_up(lo).start()

            to_y(lo).start()
            to_core(lo, y).start()

        @pl.when(has_hi & (s > 0))
        def _():
            to_dn(hi).wait_recv()

            @pl.when(has_dn)
            def _():
                to_dn(hi).start()

            to_y(hi).start()
            to_core(hi, y).start()

        @pl.when(has_lo_y)
        def _():
            from_y(lo_y).wait_recv()
            to_core(lo_y, 1 - y).start()

        @pl.when(has_hi_y)
        def _():
            from_y(hi_y).wait_recv()
            to_core(hi_y, 1 - y).start()

        def take(q, carry_q):
            side, late = q % 2, q // 2
            dist = s - late
            o = z + (2 * side - 1) * dist
            yy = y + late * (1 - 2 * y)

            @pl.when((o >= 0) & (o < depth) & ((dist > 0) | (side == 0)))
            def _():
                from_core(o, yy).wait_recv()
                absorb(o, yy)

            return carry_q

        return lax.fori_loop(0, 4, take, carry)

    from_core(z, y).wait_recv()
    absorb(z, y)
    lax.fori_loop(1, depth + 1, step, 0)

    def drain(o, carry):
        to_y(o).wait_send()
        to_core(o, 0).wait_send()
        to_core(o, 1).wait_send()

        @pl.when(has_up & (o <= z))
        def _():
            to_up(o).wait_send()

        @pl.when(has_dn & (o >= z))
        def _():
            to_dn(o).wait_send()

        return carry

    lax.fori_loop(0, depth, drain, 0)

    total = tot_sc[...]
    mean_ref[...] = sum_sc[0:nparam, :] / total
    lev_ref[...] = max_sc[...] + jnp.log(total)


def solution(mesh):
    depth = mesh.shape["blk"] // 4

    def on_device(observed, sharpness, obs_class, pattern, evolved, sim_params, sim_class):
        rows, feat = observed.shape
        sims = evolved.shape[0]
        nparam = sim_params.shape[0]
        packet_rows = feat // LANES * sims + AUX_ROWS
        vmem = pl.BlockSpec(memory_space=pltpu.VMEM)
        hbm = pl.BlockSpec(memory_space=pltpu.HBM)
        dma = pltpu.SemaphoreType.DMA
        mean, lev = pl.pallas_call(
            functools.partial(kernel, depth),
            out_shape=(
                jax.ShapeDtypeStruct((nparam, rows), jnp.float32),
                jax.ShapeDtypeStruct((1, rows), jnp.float32),
            ),
            in_specs=[hbm, vmem, vmem, pl.BlockSpec(memory_space=pltpu.SMEM), hbm, vmem, vmem],
            out_specs=(vmem, vmem),
            scratch_shapes=[
                pltpu.VMEM((depth, 2, 2, packet_rows, LANES), jnp.bfloat16),
                pltpu.VMEM((rows, feat), jnp.bfloat16),
                pltpu.VMEM((sims, feat), jnp.bfloat16),
                pltpu.VMEM((AUX_ROWS, LANES), jnp.float32),
                pltpu.VMEM((1, rows), jnp.float32),
                pltpu.VMEM((1, rows), jnp.float32),
                pltpu.VMEM((1, rows), jnp.float32),
                pltpu.VMEM((AUX_ROWS, rows), jnp.float32),
                dma((2,)),
                dma((depth,)),
                dma((depth,)),
                dma((depth,)),
                dma((2 * depth,)),
                dma((depth,)),
                dma((depth,)),
                dma((2 * depth,)),
            ],
            compiler_params=pltpu.CompilerParams(
                collective_id=0, has_side_effects=True, vmem_limit_bytes=40 << 20
            ),
        )(
            observed,
            sharpness.reshape(1, rows),
            obs_class.reshape(1, rows),
            pattern,
            evolved,
            sim_params,
            sim_class.reshape(1, sims),
        )
        return mean, lev.reshape(rows)

    placed = (
        P(("parts", "blk"), None),
        P(("parts", "blk")),
        P(("parts", "blk")),
        P(("parts", "blk"), None),
        P(("parts", "blk"), None),
        P(None, ("parts", "blk")),
        P(("parts", "blk")),
    )
    return jax.shard_map(
        on_device,
        mesh=mesh,
        in_specs=placed,
        out_specs=(P(None, ("parts", "blk")), P(("parts", "blk"))),
        check_vma=False,
    )
```

time: 162 us -> 42.5 us (0.26)
  the two profiles are of different devices: /device:TPU:0 before, /device:TPU:1 now
where the time goes in v1:
time: 42.5 us; the launch traced here: 42.2 us
  Pallas kernels  34.6 us (81%)
  local copies, waits for them, and re-layouts  6.35 us (15%)
  between operations  0.64 us (2%)
  other arithmetic  0.61 us (1%)
    pallas_call x1, Pallas kernels, on_device(): pl.pallas_call(functools.partial(kernel, depth), out_shape=(jax.ShapeDtyp...  34.6 us
    unnamed x11, local copies, waits for them, and re-layouts  4.98 us

profile of v1, /device:TPU:1, one launch (start us, length us, event | category | flops | bytes accessed | tf_op | source)
XLA Modules:
  0.0 42.2 jit_solution(5254069941826997748)
XLA Ops:
  0.6 0.7 %reshape.16.sharp_ref = f32[1,768]{1,0:T(1,128)S(1)} reshape(f32[768]{0:T(1024)} %param.8) | data formatting | bytes 6144 | tf_op jit(solution)/shard_map/reshape | solution.py:325
  1.3 0.7 %reshape.17.ocls_ref = s32[1,768]{1,0:T(1,128)S(1)} reshape(s32[768]{0:T(1024)} %param.9) | data formatting | bytes 6144 | tf_op jit(solution)/shard_map/reshape | solution.py:326
  2.0 0.0 copy-start
  2.0 1.4 %copy-done = bf16[768,1024]{1,0:T(8,128)(2,1)S(1)} copy-done((bf16[768,1024]{1,0:T(8,128)(2,1)S(1)}, bf16[768,1024]{1,0:T(8,128)(2,1)}, u32[]{:S(2)}) %copy-start) | copy-done | bytes 1572888
  3.4 0.0 copy-start.1
  3.4 0.9 %copy-done.1 = bf16[128,1024]{1,0:T(8,128)(2,1)S(1)} copy-done((bf16[128,1024]{1,0:T(8,128)(2,1)S(1)}, bf16[128,1024]{1,0:T(8,128)(2,1)}, u32[]{:S(2)}) %copy-start.1) | copy-done | bytes 262168
  4.4 0.0 copy-start.2
  4.4 0.7 %copy-done.2 = s32[6,16]{1,0:T(8,128)S(1)} copy-done((s32[6,16]{1,0:T(8,128)S(1)}, s32[6,16]{1,0:T(8,128)}, u32[]{:S(2)}) %copy-start.2) | copy-done | bytes 408
  5.1 0.0 copy-start.3
  5.1 0.7 %copy-done.3 = bf16[4,128]{1,0:T(4,128)(2,1)S(1)} copy-done((bf16[4,128]{1,0:T(4,128)(2,1)S(1)}, bf16[4,128]{1,0:T(4,128)(2,1)}, u32[]{:S(2)}) %copy-start.3) | copy-done | bytes 1048
  5.7 0.0 copy-start.4
  5.7 0.7 %copy-done.4 = s32[128]{0:T(128)S(1)} copy-done((s32[128]{0:T(128)S(1)}, s32[128]{0:T(128)}, u32[]{:S(2)}) %copy-start.4) | copy-done | bytes 536
  6.4 34.6 %shard_map.86 = (f32[4,768]{1,0:T(4,128)S(1)}, f32[1,768]{1,0:T(1,128)S(1)}) custom-call(bf16[768,1024]{1,0:T(8,128)(2,1)S(1)} %copy-done, f32[1,768]{1,0:T(1,128)S(1)} %reshape.16.sharp_ref, s32[1,768]{1,0:T(1,128)S(1)} %reshape.17.ocls_ref, s32[6,16]{1,0:T(8,128)S(1)} %copy-done.2, bf16[128,1024]{1,0:T(8,128)(2,1)S(1)} %copy-done.1, ...), custom_call_target="tpu_custom_call" | custom-call | tf_op jit(solution)/shard_map/pallas_call | solution.py:294
  41.0 0.6 %reduce = f32[768]{0:T(1024)} reduce(f32[1,768]{1,0:T(1,128)S(1)} %get-tuple-element.5, f32[]{:T(128)} %constant.1), dimensions={0}, to_apply=%get-tuple-element.5.reduce_sub_computation | reduce | bytes 6148 | tf_op jit(solution)/shard_map/pallas_call | solution.py:294
  41.6 0.6 %copy.10 = f32[4,768]{1,0:T(4,128)} copy(f32[4,768]{1,0:T(4,128)S(1)} %get-tuple-element.8) | data formatting | bytes 24576
Async XLA Ops:
  2.0 1.4 %copy-start = (bf16[768,1024]{1,0:T(8,128)(2,1)S(1)}, bf16[768,1024]{1,0:T(8,128)(2,1)}, u32[]{:S(2)}) copy-start(bf16[768,1024]{1,0:T(8,128)(2,1)} %obs_hbm.1) | copy-start | bytes 4718596
  3.4 0.9 %copy-start.1 = (bf16[128,1024]{1,0:T(8,128)(2,1)S(1)}, bf16[128,1024]{1,0:T(8,128)(2,1)}, u32[]{:S(2)}) copy-start(bf16[128,1024]{1,0:T(8,128)(2,1)} %evo_hbm.1) | copy-start | bytes 786436
  4.4 0.7 %copy-start.2 = (s32[6,16]{1,0:T(8,128)S(1)}, s32[6,16]{1,0:T(8,128)}, u32[]{:S(2)}) copy-start(s32[6,16]{1,0:T(8,128)} %pat_ref.1) | copy-start | bytes 1156
  5.1 0.7 %copy-start.3 = (bf16[4,128]{1,0:T(4,128)(2,1)S(1)}, bf16[4,128]{1,0:T(4,128)(2,1)}, u32[]{:S(2)}) copy-start(bf16[4,128]{1,0:T(4,128)(2,1)} %prm_ref.1) | copy-start | bytes 3076
  5.7 0.7 %copy-start.4 = (s32[128]{0:T(128)S(1)}, s32[128]{0:T(128)}, u32[]{:S(2)}) copy-start(s32[128]{0:T(128)} %param.13) | copy-start | bytes 1540

commit v2 on v1

--- a/solution.py
+++ b/solution.py
@@ -17,18 +17,25 @@
 def kernel(
     depth,
     obs_hbm,
-    sharp_ref,
-    ocls_ref,
-    pat_ref,
+    sharp_hbm,
+    ocls_hbm,
+    pat_hbm,
     evo_hbm,
-    prm_ref,
-    scls_ref,
+    prm_hbm,
+    scls_hbm,
     mean_ref,
     lev_ref,
     gat,
     obs,
     evo,
+    sharp_in,
+    ocls_in,
+    pat_ref,
+    prm_ref,
+    scls_in,
     stage,
+    sharp_ref,
+    ocls_ref,
     base_sc,
     max_sc,
     tot_sc,
@@ -47,17 +54,22 @@
     rows, feat = obs.shape
     sims = evo.shape[0]
     tiles = feat // LANES
-    tile_count = pat_ref.shape[0]
+    tile_count = pat_hbm.shape[0]
     tile_rows = rows // tile_count
-    nparam = prm_ref.shape[0]
+    nparam = prm_hbm.shape[0]
 
     def blk_of(zz, yy, cc):
         return zz * 4 + yy * 2 + cc
 
     evo_copy = pltpu.make_async_copy(evo_hbm, evo, local_sem.at[0])
-    obs_copy = pltpu.make_async_copy(obs_hbm, obs, local_sem.at[1])
-    evo_copy.start()
-    obs_copy.start()
+    prm_copy = pltpu.make_async_copy(prm_hbm, prm_ref, local_sem.at[1])
+    scls_copy = pltpu.make_async_copy(scls_hbm, scls_in, local_sem.at[2])
+    obs_copy = pltpu.make_async_copy(obs_hbm, obs, local_sem.at[3])
+    sharp_copy = pltpu.make_async_copy(sharp_hbm, sharp_in, local_sem.at[4])
+    ocls_copy = pltpu.make_async_copy(ocls_hbm, ocls_in, local_sem.at[5])
+    pat_copy = pltpu.make_async_copy(pat_hbm, pat_ref, local_sem.at[6])
+    for copy in (evo_copy, prm_copy, scls_copy, obs_copy, sharp_copy, ocls_copy, pat_copy):
+        copy.start()
 
     has_up = z < depth - 1
     has_dn = z > 0
@@ -79,8 +91,10 @@
         greet(blk_of(z - 1, y, c))
 
     stage[...] = jnp.zeros_like(stage)
+    prm_copy.wait()
     stage[0:nparam, :] = prm_ref[...].astype(jnp.float32)
-    stage[nparam : nparam + 1, :] = scls_ref[...].astype(jnp.float32)
+    scls_copy.wait()
+    stage[nparam : nparam + 1, :] = scls_in[...].reshape(1, sims).astype(jnp.float32)
     evo_copy.wait()
     for t in range(tiles):
         gat[z, y, c, t * sims : (t + 1) * sims, :] = evo[:, t * LANES : (t + 1) * LANES]
@@ -132,8 +146,14 @@
     to_y(z).start()
     to_core(z, y).start()
 
+    sharp_copy.wait()
+    ocls_copy.wait()
+    pat_copy.wait()
     obs_copy.wait()
     for i in range(rows // LANES):
+        lanes = slice(i * LANES, (i + 1) * LANES)
+        sharp_ref[0:1, lanes] = 2.0 * sharp_in[lanes].reshape(1, LANES)
+        ocls_ref[0:1, lanes] = ocls_in[lanes].reshape(1, LANES)
         part = obs[i * LANES : (i + 1) * LANES, :].astype(jnp.float32)
         col = jnp.sum(part * part, axis=1, keepdims=True)
         wide = jnp.broadcast_to(col, (LANES, LANES)).T
@@ -165,7 +185,7 @@
             inner = lax.dot_general(
                 lhs, obs[span, :], (((1,), (1,)), ((), ())), preferred_element_type=jnp.float32
             )
-            sharp2 = 2.0 * sharp_ref[0:1, span]
+            sharp2 = sharp_ref[0:1, span]
             base = base_sc[0:1, span]
             masked = []
             for cc in range(2):
@@ -277,7 +297,10 @@
 
     total = tot_sc[...]
     mean_ref[...] = sum_sc[0:nparam, :] / total
-    lev_ref[...] = max_sc[...] + jnp.log(total)
+    lev = max_sc[...] + jnp.log(total)
+    for i in range(rows // LANES):
+        lanes = slice(i * LANES, (i + 1) * LANES)
+        lev_ref[lanes] = lev[0:1, lanes].reshape(LANES)
 
 
 def solution(mesh):
@@ -295,20 +318,27 @@
             functools.partial(kernel, depth),
             out_shape=(
                 jax.ShapeDtypeStruct((nparam, rows), jnp.float32),
-                jax.ShapeDtypeStruct((1, rows), jnp.float32),
+                jax.ShapeDtypeStruct((rows,), jnp.float32),
             ),
-            in_specs=[hbm, vmem, vmem, pl.BlockSpec(memory_space=pltpu.SMEM), hbm, vmem, vmem],
+            in_specs=[hbm] * 7,
             out_specs=(vmem, vmem),
             scratch_shapes=[
                 pltpu.VMEM((depth, 2, 2, packet_rows, LANES), jnp.bfloat16),
                 pltpu.VMEM((rows, feat), jnp.bfloat16),
                 pltpu.VMEM((sims, feat), jnp.bfloat16),
+                pltpu.VMEM((rows,), jnp.float32),
+                pltpu.VMEM((rows,), jnp.int32),
+                pltpu.SMEM(pattern.shape, jnp.int32),
+                pltpu.VMEM((nparam, sims), jnp.bfloat16),
+                pltpu.VMEM((sims,), jnp.int32),
                 pltpu.VMEM((AUX_ROWS, LANES), jnp.float32),
+                pltpu.VMEM((1, rows), jnp.float32),
+                pltpu.VMEM((1, rows), jnp.int32),
                 pltpu.VMEM((1, rows), jnp.float32),
                 pltpu.VMEM((1, rows), jnp.float32),
                 pltpu.VMEM((1, rows), jnp.float32),
                 pltpu.VMEM((AUX_ROWS, rows), jnp.float32),
-                dma((2,)),
+                dma((7,)),
                 dma((depth,)),
                 dma((depth,)),
                 dma((depth,)),
@@ -318,18 +348,18 @@
                 dma((2 * depth,)),
             ],
             compiler_params=pltpu.CompilerParams(
-                collective_id=0, has_side_effects=True, vmem_limit_bytes=40 << 20
+                collective_id=0, has_side_effects=True, vmem_limit_bytes=60 << 20
             ),
         )(
             observed,
-            sharpness.reshape(1, rows),
-            obs_class.reshape(1, rows),
+            sharpness,
+            obs_class,
             pattern,
             evolved,
             sim_params,
-            sim_class.reshape(1, sims),
+            sim_class,
         )
-        return mean, lev.reshape(rows)
+        return mean, lev
 
     placed = (
         P(("parts", "blk"), None),

time: 42.5 us -> 37.7 us (0.89)
  local copies, waits for them, and re-layouts: 6.35 us -> 2.57 us
  other arithmetic: 0.61 us -> 0 us
    unnamed x11 -> x2, local copies, waits for them, and re-layouts: 4.98 us -> 2.57 us
    reshape x2 -> x0, local copies, waits for them, and re-layouts: 1.38 us -> none  [the longest x1 0.69 us: on_device(): sharpness.reshape(1, rows)]
    pallas_call x1 -> x0, other arithmetic: 0.61 us -> none  [on_device(): pl.pallas_call(functools.partial(kernel, depth), out_shape=(jax.ShapeDtyp...]
where the time goes in v2:
time: 37.7 us; the launch traced here: 37.4 us
  Pallas kernels  34.2 us (91%)
  local copies, waits for them, and re-layouts  2.57 us (7%)
  between operations  0.64 us (2%)
    pallas_call x1, Pallas kernels, on_device(): pl.pallas_call(functools.partial(kernel, depth), out_shape=(jax.ShapeDtyp...  34.2 us
    unnamed x2, local copies, waits for them, and re-layouts  2.57 us

profile of v2, /device:TPU:1, one launch (start us, length us, event | category | flops | bytes accessed | tf_op | source)
XLA Modules:
  0.0 37.4 jit_solution(12806701652754968005)
XLA Ops:
  0.6 34.2 %shard_map.86 = (f32[4,768]{1,0:T(4,128)}, f32[768]{0:T(1024)}) custom-call(bf16[768,1024]{1,0:T(8,128)(2,1)} %obs_hbm.1, f32[768]{0:T(1024)} %sharp_hbm.1, s32[768]{0:T(1024)} %ocls_hbm.1, s32[6,16]{1,0:T(8,128)} %pat_hbm.1, bf16[128,1024]{1,0:T(8,128)(2,1)} %evo_hbm.1, bf16[4,128]{1,0:T(4,128)(2,1)} %prm_hbm.1, s32[128]{0:T(128)} %scls_hbm.1), custom_call_target="tpu_custom_call" | custom-call | tf_op jit(solution)/shard_map/pallas_call | solution.py:317
  34.9 1.3 %copy.11 = f32[4,768]{1,0:T(4,128)} copy(f32[4,768]{1,0:T(4,128)} %get-tuple-element.4) | data formatting | bytes 24576
  36.2 1.3 %copy.12 = f32[768]{0:T(1024)} copy(f32[768]{0:T(1024)} %get-tuple-element.5) | data formatting | bytes 6144

commit v3 on v2

--- a/solution.py
+++ b/solution.py
@@ -11,6 +11,7 @@
 NEG_MASK = -3e38
 LANES = 128
 AUX_ROWS = 16
+LATE = 2
 MESH = pl.DeviceIdType.MESH
 
 
@@ -73,6 +74,7 @@
 
     has_up = z < depth - 1
     has_dn = z > 0
+    inner = ((z + depth - 1) // depth) * ((2 * depth - 2 - z) // depth)
 
     barrier = pltpu.get_barrier_semaphore()
 
@@ -103,48 +105,77 @@
     peers = 2 + (z + depth - 1) // depth + (2 * depth - 2 - z) // depth
     pl.semaphore_wait(barrier, peers)
 
-    def packet(o, yy, cc, dev, send, recv):
+    total_rows = gat.shape[3]
+    early = (total_rows + 95) // 96 * 16
+    cuts = [early + (total_rows - early) * k // (16 * LATE) * 16 for k in range(LATE)] + [total_rows]
+    pieces = [(cuts[k], cuts[k + 1] - cuts[k]) for k in range(LATE)] + [(0, early)]
+
+    def hop(o, yy, k, dev, send, recv):
+        ref = gat.at[o, yy, c, pl.ds(*pieces[k])]
         return pltpu.make_async_remote_copy(
-            src_ref=gat.at[o, yy, cc],
-            dst_ref=gat.at[o, yy, cc],
+            src_ref=ref,
+            dst_ref=ref,
             send_sem=send,
             recv_sem=recv,
             device_id={"blk": dev},
             device_id_type=MESH,
         )
 
-    def to_up(o):
-        return packet(o, y, c, blk_of(z + 1, y, c), up_send.at[o], z_recv.at[o])
-
-    def to_dn(o):
-        return packet(o, y, c, blk_of(z - 1, y, c), dn_send.at[o], z_recv.at[o])
-
-    def to_y(o):
-        return packet(o, y, c, blk_of(z, 1 - y, c), y_send.at[o], y_recv.at[o])
-
-    def from_y(o):
-        return packet(o, 1 - y, c, blk_of(z, 1 - y, c), y_send.at[o], y_recv.at[o])
-
-    def to_core(o, yy):
-        return packet(
-            o, yy, c, blk_of(z, y, 1 - c), s_send.at[o * 2 + yy], s_recv.at[o * 2 + yy]
+    def along_z(o, j, zz, send):
+        yy, k = (y, j) if j <= LATE else (1 - y, LATE)
+        slot = o * (LATE + 2) + j
+        return hop(o, yy, k, blk_of(zz, y, c), send.at[slot], z_recv.at[slot])
+
+    def to_up(o, j):
+        return along_z(o, j, z + 1, up_send)
+
+    def to_dn(o, j):
+        return along_z(o, j, z - 1, dn_send)
+
+    def across_y(o, yy, k):
+        slot = o * (LATE + 1) + k
+        return hop(o, yy, k, blk_of(z, 1 - y, c), y_send.at[slot], y_recv.at[slot])
+
+    def to_y(o, k):
+        return across_y(o, y, k)
+
+    def from_y(o, k):
+        return across_y(o, 1 - y, k)
+
+    def core_hop(o, yy, cc, part):
+        span = pl.ds(0, early) if part else pl.ds(early, total_rows - early)
+        ref = gat.at[o, yy, cc, span]
+        slot = (o * 2 + yy) * 2 + part
+        return pltpu.make_async_remote_copy(
+            src_ref=ref,
+            dst_ref=ref,
+            send_sem=s_send.at[slot],
+            recv_sem=s_recv.at[slot],
+            device_id={"blk": blk_of(z, y, 1 - c)},
+            device_id_type=MESH,
         )
 
-    def from_core(o, yy):
-        return packet(
-            o, yy, 1 - c, blk_of(z, y, 1 - c), s_send.at[o * 2 + yy], s_recv.at[o * 2 + yy]
-        )
-
-    @pl.when(has_up)
-    def _():
-        to_up(z).start()
-
-    @pl.when(has_dn)
-    def _():
-        to_dn(z).start()
-
-    to_y(z).start()
-    to_core(z, y).start()
+    def to_core(o, yy, part):
+        return core_hop(o, yy, c, part)
+
+    def from_core(o, yy, part):
+        return core_hop(o, yy, 1 - c, part)
+
+    def own_both_ways(j):
+        @pl.when(has_up)
+        def _():
+            to_up(z, j).start()
+
+        @pl.when(has_dn)
+        def _():
+            to_dn(z, j).start()
+
+    to_y(z, LATE).start()
+    for j in range(LATE):
+        own_both_ways(j)
+        to_y(z, j).start()
+    to_core(z, y, 0).start()
+    to_core(z, y, 1).start()
 
     sharp_copy.wait()
     ocls_copy.wait()
@@ -182,7 +213,7 @@
         lhs = jnp.concatenate(lhs, axis=0)
         for g in range(tile_count // group):
             span = slice(g * width, (g + 1) * width)
-            inner = lax.dot_general(
+            product = lax.dot_general(
                 lhs, obs[span, :], (((1,), (1,)), ((), ())), preferred_element_type=jnp.float32
             )
             sharp2 = sharp_ref[0:1, span]
@@ -200,7 +231,7 @@
                     ],
                     axis=1,
                 ).astype(jnp.float32)
-                score = ((inner[cc * sims : (cc + 1) * sims] - half_sq[cc]) + base) * sharp2
+                score = ((product[cc * sims : (cc + 1) * sims] - half_sq[cc]) + base) * sharp2
                 masked.append(jnp.where(classes[cc] == wanted, score, NEG_MASK))
             top = jnp.max(jnp.maximum(masked[0], masked[1]), axis=0, keepdims=True)
             old = max_sc[0:1, span]
@@ -221,78 +252,91 @@
             sum_sc[:, span] = sum_sc[:, span] * factor + added
 
     def step(s, carry):
-        lo, hi = z - s, z + s
-        has_lo, has_hi = lo >= 0, hi < depth
-        lo_y, hi_y = z - s + 1, z + s - 1
-        has_lo_y = lo_y >= 0
-        has_hi_y = (hi_y < depth) & (s > 1)
-
-        @pl.when(has_lo)
+        def sides(dist):
+            lo, hi = z - dist, z + dist
+            return ((lo, lo >= 0, has_up, to_up), (hi, (hi < depth) & (dist > 0), has_dn, to_dn))
+
+        for j in range(LATE):
+            for o, there, further, to in sides(s):
+
+                @pl.when(there)
+                def _():
+                    to(o, j).wait_recv()
+
+                    @pl.when(further)
+                    def _():
+                        to(o, j).start()
+
+                    to_y(o, j).start()
+                    if j == LATE - 1:
+                        to_core(o, y, 0).start()
+
+        @pl.when(s == 1)
         def _():
-            to_up(lo).wait_recv()
-
-            @pl.when(has_up)
+            own_both_ways(LATE)
+            from_y(z, LATE).wait_recv()
+            own_both_ways(LATE + 1)
+            to_core(z, 1 - y, 1).start()
+
+        for j, yy in ((LATE, y), (LATE + 1, 1 - y)):
+            for o, there, further, to in sides(s - 1):
+
+                @pl.when(there & (s > 1))
+                def _():
+                    to(o, j).wait_recv()
+
+                    @pl.when(further)
+                    def _():
+                        to(o, j).start()
+
+                    to_core(o, yy, 1).start()
+
+        done = s - 1 - inner
+
+        for o, there, further, to in sides(done):
+
+            @pl.when(there & (done >= 0))
             def _():
-                to_up(lo).start()
-
-            to_y(lo).start()
-            to_core(lo, y).start()
-
-        @pl.when(has_hi & (s > 0))
-        def _():
-            to_dn(hi).wait_recv()
-
-            @pl.when(has_dn)
+                for k in range(LATE):
+                    from_y(o, k).wait_recv()
+                to_core(o, 1 - y, 0).start()
+
+        def pick(q, carry_q):
+            side, other = q % 2, q // 2
+            o = z + (2 * side - 1) * done
+            yy = y + other * (1 - 2 * y)
+
+            @pl.when((o >= 0) & (o < depth) & (done >= 0) & ((done > 0) | (side == 0)))
             def _():
-                to_dn(hi).start()
-
-            to_y(hi).start()
-            to_core(hi, y).start()
-
-        @pl.when(has_lo_y)
-        def _():
-            from_y(lo_y).wait_recv()
-            to_core(lo_y, 1 - y).start()
-
-        @pl.when(has_hi_y)
-        def _():
-            from_y(hi_y).wait_recv()
-            to_core(hi_y, 1 - y).start()
-
-        def take(q, carry_q):
-            side, late = q % 2, q // 2
-            dist = s - late
-            o = z + (2 * side - 1) * dist
-            yy = y + late * (1 - 2 * y)
-
-            @pl.when((o >= 0) & (o < depth) & ((dist > 0) | (side == 0)))
+                from_core(o, yy, 0).wait_recv()
+                from_core(o, yy, 1).wait_recv()
+                absorb(o, yy)
+
+            return carry_q
+
+        return lax.fori_loop(0, 4, pick, carry)
+
+    lax.fori_loop(1, depth + 1, step, 0)
+
+    def drain(o, carry):
+        for part in range(2):
+            to_core(o, 0, part).wait_send()
+            to_core(o, 1, part).wait_send()
+        for k in range(LATE):
+            to_y(o, k).wait_send()
+        for j in range(LATE + 2):
+
+            @pl.when(has_up & (o <= z))
             def _():
-                from_core(o, yy).wait_recv()
-                absorb(o, yy)
-
-            return carry_q
-
-        return lax.fori_loop(0, 4, take, carry)
-
-    from_core(z, y).wait_recv()
-    absorb(z, y)
-    lax.fori_loop(1, depth + 1, step, 0)
-
-    def drain(o, carry):
-        to_y(o).wait_send()
-        to_core(o, 0).wait_send()
-        to_core(o, 1).wait_send()
-
-        @pl.when(has_up & (o <= z))
-        def _():
-            to_up(o).wait_send()
-
-        @pl.when(has_dn & (o >= z))
-        def _():
-            to_dn(o).wait_send()
+                to_up(o, j).wait_send()
+
+            @pl.when(has_dn & (o >= z))
+            def _():
+                to_dn(o, j).wait_send()
 
         return carry
 
+    to_y(z, LATE).wait_send()
     lax.fori_loop(0, depth, drain, 0)
 
     total = tot_sc[...]
@@ -339,13 +383,13 @@
                 pltpu.VMEM((1, rows), jnp.float32),
                 pltpu.VMEM((AUX_ROWS, rows), jnp.float32),
                 dma((7,)),
-                dma((depth,)),
-                dma((depth,)),
-                dma((depth,)),
-                dma((2 * depth,)),
-                dma((depth,)),
-                dma((depth,)),
-                dma((2 * depth,)),
+                dma(((LATE + 2) * depth,)),
+                dma(((LATE + 2) * depth,)),
+                dma(((LATE + 1) * depth,)),
+                dma((4 * depth,)),
+                dma(((LATE + 2) * depth,)),
+                dma(((LATE + 1) * depth,)),
+                dma((4 * depth,)),
             ],
             compiler_params=pltpu.CompilerParams(
                 collective_id=0, has_side_effects=True, vmem_limit_bytes=60 << 20

time: 37.7 us -> 36.4 us (0.966); the launches traced: 37.4 us -> 35.7 us
  Pallas kernels: 34.2 us -> 32.5 us
    pallas_call x1, Pallas kernels: 34.2 us -> 32.5 us  [on_device(): pl.pallas_call(functools.partial(kernel, depth), out_shape=(jax.ShapeDtyp...]
where the time goes in v3:
time: 36.4 us; the launch traced here: 35.7 us
  Pallas kernels  32.5 us (89%)
  local copies, waits for them, and re-layouts  2.57 us (7%)
  between operations  0.64 us (2%)
    pallas_call x1, Pallas kernels, on_device(): pl.pallas_call(functools.partial(kernel, depth), out_shape=(jax.ShapeDtyp...  32.5 us
    unnamed x2, local copies, waits for them, and re-layouts  2.57 us

profile of v3, /device:TPU:1, one launch (start us, length us, event | category | flops | bytes accessed | tf_op | source)
XLA Modules:
  0.0 35.7 jit_solution(3420256557278673639)
XLA Ops:
  0.6 32.5 %shard_map.86 = (f32[4,768]{1,0:T(4,128)}, f32[768]{0:T(1024)}) custom-call(bf16[768,1024]{1,0:T(8,128)(2,1)} %obs_hbm.1, f32[768]{0:T(1024)} %sharp_hbm.1, s32[768]{0:T(1024)} %ocls_hbm.1, s32[6,16]{1,0:T(8,128)} %pat_hbm.1, bf16[128,1024]{1,0:T(8,128)(2,1)} %evo_hbm.1, bf16[4,128]{1,0:T(4,128)(2,1)} %prm_hbm.1, s32[128]{0:T(128)} %scls_hbm.1), custom_call_target="tpu_custom_call" | custom-call | tf_op jit(solution)/shard_map/pallas_call | solution.py:361
  33.2 1.3 %copy.11 = f32[4,768]{1,0:T(4,128)} copy(f32[4,768]{1,0:T(4,128)} %get-tuple-element.4) | data formatting | bytes 24576
  34.5 1.3 %copy.12 = f32[768]{0:T(1024)} copy(f32[768]{0:T(1024)} %get-tuple-element.5) | data formatting | bytes 6144

commit v4 on v3

--- a/solution.py
+++ b/solution.py
@@ -11,7 +11,7 @@
 NEG_MASK = -3e38
 LANES = 128
 AUX_ROWS = 16
-LATE = 2
+LATE = 3
 MESH = pl.DeviceIdType.MESH
 
 
@@ -98,6 +98,13 @@
     scls_copy.wait()
     stage[nparam : nparam + 1, :] = scls_in[...].reshape(1, sims).astype(jnp.float32)
     evo_copy.wait()
+    own = evo[...].astype(jnp.float32)
+    own_sq = 0.5 * jnp.sum(own * own, axis=1, keepdims=True)
+    left = jnp.broadcast_to(own_sq, (LANES, LANES)).T[0:1, :]
+    for k in range(3):
+        part = left.astype(jnp.bfloat16).astype(jnp.float32)
+        stage[nparam + 1 + k : nparam + 2 + k, :] = part
+        left = left - part
     for t in range(tiles):
         gat[z, y, c, t * sims : (t + 1) * sims, :] = evo[:, t * LANES : (t + 1) * LANES]
     gat[z, y, c, tiles * sims : tiles * sims + AUX_ROWS, :] = stage[...].astype(jnp.bfloat16)
@@ -193,7 +200,7 @@
     max_sc[...] = jnp.full_like(max_sc, NEG_START)
     tot_sc[...] = jnp.zeros_like(tot_sc)
     sum_sc[...] = jnp.zeros_like(sum_sc)
-    group = 2 if tile_count % 2 == 0 else 1
+    group = tile_count
     width = group * tile_rows
 
     def absorb(o, yy):
@@ -202,12 +209,16 @@
             block = jnp.concatenate(
                 [gat[o, yy, cc, t * sims : (t + 1) * sims, :] for t in range(tiles)], axis=1
             )
-            wide = block.astype(jnp.float32)
-            half_sq.append(0.5 * jnp.sum(wide * wide, axis=1, keepdims=True))
             extra = gat[o, yy, cc, tiles * sims : tiles * sims + AUX_ROWS, :]
-            row = extra.astype(jnp.float32)[nparam : nparam + 1, :]
-            turned = jnp.broadcast_to(row, (LANES, LANES)).T
-            classes.append(turned[:, 0:1])
+            rows_f32 = extra.astype(jnp.float32)
+            row = rows_f32[nparam : nparam + 1, :]
+            row_sq = (
+                rows_f32[nparam + 1 : nparam + 2, :]
+                + rows_f32[nparam + 2 : nparam + 3, :]
+                + rows_f32[nparam + 3 : nparam + 4, :]
+            )
+            classes.append(jnp.broadcast_to(row, (LANES, LANES)).T[:, 0:1])
+            half_sq.append(jnp.broadcast_to(row_sq, (LANES, LANES)).T[:, 0:1])
             aux.append(extra)
             lhs.append(block)
         lhs = jnp.concatenate(lhs, axis=0)

time: 36.4 us -> 34.9 us (0.959)
  Pallas kernels: 32.5 us -> 31.3 us
    pallas_call x1, Pallas kernels: 32.5 us -> 31.3 us  [on_device(): pl.pallas_call(functools.partial(kernel, depth), out_shape=(jax.ShapeDtyp...]
where the time goes in v4:
time: 34.9 us; the launch traced here: 34.5 us
  Pallas kernels  31.3 us (90%)
  local copies, waits for them, and re-layouts  2.57 us (7%)
  between operations  0.64 us (2%)
    pallas_call x1, Pallas kernels, on_device(): pl.pallas_call(functools.partial(kernel, depth), out_shape=(jax.ShapeDtyp...  31.3 us
    unnamed x2, local copies, waits for them, and re-layouts  2.57 us

profile of v4, /device:TPU:1, one launch (start us, length us, event | category | flops | bytes accessed | tf_op | source)
XLA Modules:
  0.0 34.5 jit_solution(16306168390586690058)
XLA Ops:
  0.6 31.3 %shard_map.86 = (f32[4,768]{1,0:T(4,128)}, f32[768]{0:T(1024)}) custom-call(bf16[768,1024]{1,0:T(8,128)(2,1)} %obs_hbm.1, f32[768]{0:T(1024)} %sharp_hbm.1, s32[768]{0:T(1024)} %ocls_hbm.1, s32[6,16]{1,0:T(8,128)} %pat_hbm.1, bf16[128,1024]{1,0:T(8,128)(2,1)} %evo_hbm.1, bf16[4,128]{1,0:T(4,128)(2,1)} %prm_hbm.1, s32[128]{0:T(128)} %scls_hbm.1), custom_call_target="tpu_custom_call" | custom-call | tf_op jit(solution)/shard_map/pallas_call | solution.py:372
  31.9 1.3 %copy.11 = f32[4,768]{1,0:T(4,128)} copy(f32[4,768]{1,0:T(4,128)} %get-tuple-element.4) | data formatting | bytes 24576
  33.2 1.3 %copy.12 = f32[768]{0:T(1024)} copy(f32[768]{0:T(1024)} %get-tuple-element.5) | data formatting | bytes 6144
